TPU v7x, 128 devices: a whole 4x4x4 slice. The times are simulated.
128 devices in a mesh: shot: 4 (over y_lo, core), gx: 4 (over z), gy: 8 (over x, y_hi).
Axes of the slice: x: 4, y: 4 (y_hi: 2, y_lo: 2; y = y_hi * 2 + y_lo), z: 4, core: 2. Of those that a mesh axis runs over, the one named last changes fastest.
Arguments:
- model_tiles: float32 [256, 256, 128], P(('shot', 'gx'), 'gy'), may hold values from 0.2 to 0.45
- owner_map: int32 [16], replicated, may hold values from 0 to 15, each once
- offsets: int32 [4], P('shot'), may hold values from 0 to 12
- field_now: float32 [4, 2, 64, 256, 128], P('shot', None, 'gx', 'gy'), may hold values from -6 to 6
- field_prev: float32 [4, 2, 64, 256, 128], P('shot', None, 'gx', 'gy'), may hold values from -6 to 6
- sources: int32 [4, 2, 3], P('shot'), may hold values from 0 to 255, as said below
- wavelet: float32 [4, 2, 8], P('shot'), may hold values from -6 to 6
- receivers: int32 [4, 256, 3], P('shot'), may hold values from 0 to 255, as said below
Outputs:
- out_now: float32 [4, 2, 64, 256, 128], P('shot', None, 'gx', 'gy')
- out_prev: float32 [4, 2, 64, 256, 128], P('shot', None, 'gx', 'gy')
- traces: float32 [4, 2, 256, 8], P('shot')
Inputs may be any that keep to these rules, and one draw needn't show every extreme that they name: `sources`: each row is a cell of the group's aperture: first entry below 64, second below 256, third below 128. `receivers`: each row is a cell of the group's aperture: first entry below 64, second below 256, third below 128.
All inputs are finite; a program needn't handle non-finite values.
Results may differ from a plain program's by a relative error of at most 0.0003.
Values sent between devices are 32-bit elements; how exact they have to be, the bound alone decides.
A program may use at most 128 MiB of HBM per device.

v0:
```python
import jax
import jax.numpy as jnp
from jax import lax
from jax.sharding import PartitionSpec as P

STEPS = 8
center_weight = -2.5
near_weight = 4.0 / 3.0
far_weight = -1.0 / 12.0
damp_peak = 0.3


def extended_2(cells, sides, width):
    for axis, dim in sides:
        count = lax.axis_size(axis)
        ends = count - 1
        head = lax.slice_in_dim(cells, 0, width, axis=dim)
        tail = lax.slice_in_dim(cells, cells.shape[dim] - width, cells.shape[dim], axis=dim)
        cells = jnp.concatenate(
            [
                lax.ppermute(tail, axis, [(i, (i + 1) % count) for i in range(ends)]),
                cells,
                lax.ppermute(head, axis, [((i + 1) % count, i) for i in range(ends)]),
            ],
            axis=dim,
        )
    return cells


def depth_ahead(field, reach):
    filler = jnp.zeros(field.shape[:-1] + (reach,), field.dtype)
    return jnp.concatenate([field[..., reach:], filler], axis=-1)


def depth_behind(field, reach):
    filler = jnp.zeros(field.shape[:-1] + (reach,), field.dtype)
    return jnp.concatenate([filler, field[..., :-reach]], axis=-1)


def laplace(extended):
    middle = extended[:, 2:-2, 2:-2]
    along_x = (
        center_weight * middle
        + near_weight * (extended[:, 3:-1, 2:-2] + extended[:, 1:-3, 2:-2])
        + far_weight * (extended[:, 4:, 2:-2] + extended[:, :-4, 2:-2])
    )
    along_y = (
        center_weight * middle
        + near_weight * (extended[:, 2:-2, 3:-1] + extended[:, 2:-2, 1:-3])
        + far_weight * (extended[:, 2:-2, 4:] + extended[:, 2:-2, :-4])
    )
    along_z = (
        center_weight * middle
        + near_weight * (depth_ahead(middle, 1) + depth_behind(middle, 1))
        + far_weight * (depth_ahead(middle, 2) + depth_behind(middle, 2))
    )
    return along_x + along_y + along_z


def damping(x_cells, y_cells, width, x_total, y_total):
    x_depth = (
        jnp.maximum(width - jnp.minimum(x_cells + 1, x_total - x_cells), 0).astype(jnp.float32)
        / width
    )
    y_depth = (
        jnp.maximum(width - jnp.minimum(y_cells + 1, y_total - y_cells), 0).astype(jnp.float32)
        / width
    )
    return damp_peak * (x_depth[:, None] * x_depth[:, None] + y_depth[None, :] * y_depth[None, :])


def injection(x_cells, y_cells, z_cells, source_cells, amplitude):
    on_x = (x_cells[None, :] == source_cells[:, 0:1]).astype(jnp.float32)
    on_y = (y_cells[None, :] == source_cells[:, 1:2]).astype(jnp.float32)
    on_z = (z_cells[None, :] == source_cells[:, 2:3]).astype(jnp.float32)
    return (
        amplitude[:, None, None, None]
        * on_x[:, :, None, None]
        * on_y[:, None, :, None]
        * on_z[:, None, None, :]
    )


def advance(extended, previous, coef, damp, inject):
    middle = extended[:, 2:-2, 2:-2]
    return (2.0 * middle - (1.0 - damp) * previous + coef * laplace(extended) + inject) / (
        1.0 + damp
    )


def sample(field, receiver_cells, x_start, y_start):
    size_x, size_y = (field.shape[1], field.shape[2])
    local_x = receiver_cells[:, 0] - x_start
    local_y = receiver_cells[:, 1] - y_start
    inside = (local_x >= 0) & (local_x < size_x) & (local_y >= 0) & (local_y < size_y)
    values = field[
        :, jnp.clip(local_x, 0, size_x - 1), jnp.clip(local_y, 0, size_y - 1), receiver_cells[:, 2]
    ]
    return jnp.where(inside[None, :], values, 0.0)


def local(model_tiles, owner_map, offsets, field_now, field_prev, sources, wavelet, receivers):
    block_x, block_y, depth = model_tiles.shape
    column_index = lax.axis_index("gx")
    row_index = lax.axis_index("gy")
    across = lax.axis_size("gx")
    total_x = block_x * across
    total_y = block_y * lax.axis_size("gy")
    shift_x = offsets[0]
    tile_total = owner_map.shape[0]
    column_ids = jnp.arange(tile_total, dtype=jnp.int32)
    wanted = jnp.sum(jnp.where(column_ids == shift_x + column_index, owner_map, 0))
    piece = lax.all_gather(model_tiles, ("shot", "gx"), axis=0, tiled=True)
    rows = wanted * block_x + jnp.arange(block_x, dtype=jnp.int32)
    inside = (rows >= 0) & (rows < piece.shape[0])
    taken = jnp.take(piece, jnp.clip(rows, 0, piece.shape[0] - 1), axis=0)
    speed = jnp.where(inside[:, None, None], taken, jnp.zeros_like(model_tiles))
    coef = speed * speed
    current = field_now[0]
    previous = field_prev[0]
    source_cells = sources[0]
    amplitudes = wavelet[0]
    receiver_cells = receivers[0]
    x_start = column_index * block_x
    y_start = row_index * block_y
    x_here = x_start + jnp.arange(block_x, dtype=jnp.int32)
    y_here = y_start + jnp.arange(block_y, dtype=jnp.int32)
    z_cells = jnp.arange(depth, dtype=jnp.int32)
    damp = damping(x_here, y_here, block_x, total_x, total_y)[:, :, None]
    recorded = []
    for step in range(STEPS):
        extended = extended_2(current, (("gx", 1), ("gy", 2)), 2)
        inject = injection(x_here, y_here, z_cells, source_cells, amplitudes[:, step])
        fresh = advance(extended, previous, coef, damp, inject)
        recorded.append(sample(fresh, receiver_cells, x_start, y_start))
        previous = current
        current = fresh
    traces = lax.psum(jnp.stack(recorded, axis=-1), ("gx", "gy"))
    return (current[None], previous[None], traces[None])


def solution(mesh):
    return jax.shard_map(
        local,
        mesh=mesh,
        in_specs=(
            P(("shot", "gx"), "gy", None),
            P(),
            P("shot"),
            P("shot", None, "gx", "gy", None),
            P("shot", None, "gx", "gy", None),
            P("shot", None, None),
            P("shot", None, None),
            P("shot", None, None),
        ),
        out_specs=(
            P("shot", None, "gx", "gy", None),
            P("shot", None, "gx", "gy", None),
            P("shot", None, None, None),
        ),
        check_vma=False,
    )
```

profile of v0, /device:TPU:0, one launch (start us, length us, event | category | flops | bytes accessed | tf_op | source)
XLA Modules:
  0.0 552.9 jit_solution(16876477504030605119)
XLA Ops:
  8.8 1.3 collective-permute-start
  10.1 4.5 collective-permute-start.1
  15.3 1.3 fusion.155
  21.3 2.2 fusion.179
  23.5 2.3 fusion.178
  26.9 1.3 collective-permute-start.2
  28.2 6.1 %collective-permute-start.3 = (f32[2,20,2,128]{3,2,1,0:T(2,128)S(1)}, f32[2,20,2,128]{3,2,1,0:T(2,128)S(1)}, u32[]{:S(2)}, u32[]{:S(2)}) collective-permute-start(f32[2,20,2,128]{3,2,1,0:T(2,128)S(1)} %get-tuple-element.57), channel_id=1, source_target_pairs={{0,1},{1,2},{2,3},{3,4},{4,5},{5,6},{6,7},{8,9},{9,10},{10,11},{11... | collective-permute-start | bytes 122888 | tf_op jit(solution)/shard_map/ppermute | solution.py:21
  34.7 1.5 collective-permute-done.3
  36.1 1.4 pad_maximum_fusion
  37.5 24.6 %all-gather.2.cloned.1.call-done = f32[256,32,128]{2,1,0:T(8,128)} async-done(((f32[16,32,128]{2,1,0:T(8,128)}), f32[256,32,128]{2,1,0:T(8,128)}) %all-gather.2.cloned.1.call-update) | async-done | bytes 4194320 | tf_op jit(solution)/shard_map/all_gather | solution.py:113
  62.1 2.7 gather_fusion
  65.0 3.1 fusion.94
  68.1 1.3 collective-permute-start.4
  69.4 4.5 collective-permute-start.5
  76.1 1.3 collective-permute-start.6
  77.4 6.1 %collective-permute-start.7 = (f32[2,20,2,128]{3,2,1,0:T(2,128)S(1)}, f32[2,20,2,128]{3,2,1,0:T(2,128)S(1)}, u32[]{:S(2)}, u32[]{:S(2)}) collective-permute-start(f32[2,20,2,128]{3,2,1,0:T(2,128)S(1)} %get-tuple-element.53), channel_id=1, source_target_pairs={{0,1},{1,2},{2,3},{3,4},{4,5},{5,6},{6,7},{8,9},{9,10},{10,11},{11... | collective-permute-start | bytes 122888 | tf_op jit(solution)/shard_map/ppermute | solution.py:21
  84.4 16.7 %copy.515 = f32[2,16,32,128]{0,3,2,1:T(8,128)} copy(f32[2,16,32,128]{3,2,1,0:T(8,128)S(1)} %fusion.94) | data formatting | bytes 1048576 | tf_op jit(solution)/shard_map/div | solution.py:86
  101.0 3.0 gather_fusion.1
  104.2 2.0 fusion.82
  106.2 1.3 collective-permute-start.8
  107.5 5.0 collective-permute-start.9
  112.8 1.6 collective-permute-done.9
  114.5 1.3 collective-permute-start.10
  115.8 6.5 %collective-permute-start.11 = (f32[2,20,2,128]{3,2,1,0:T(2,128)S(1)}, f32[2,20,2,128]{3,2,1,0:T(2,128)S(1)}, u32[]{:S(2)}, u32[]{:S(2)}) collective-permute-start(f32[2,20,2,128]{3,2,1,0:T(2,128)S(1)} %get-tuple-element.49), channel_id=1, source_target_pairs={{0,1},{1,2},{2,3},{3,4},{4,5},{5,6},{6,7},{8,9},{9,10},{10,11},{11... | collective-permute-start | bytes 122888 | tf_op jit(solution)/shard_map/ppermute | solution.py:21
  123.2 16.7 %copy.516 = f32[2,16,32,128]{0,3,2,1:T(8,128)} copy(f32[2,16,32,128]{3,2,1,0:T(8,128)S(1)} %fusion.82) | data formatting | bytes 1048576 | tf_op jit(solution)/shard_map/div | solution.py:86
  139.9 3.0 gather_fusion.2
  143.1 2.0 fusion.70
  145.1 1.3 collective-permute-start.12
  146.4 4.9 collective-permute-start.13
  151.6 1.6 collective-permute-done.13
  153.2 1.3 collective-permute-start.14
  154.5 6.9 %collective-permute-start.15 = (f32[2,20,2,128]{3,2,1,0:T(2,128)S(1)}, f32[2,20,2,128]{3,2,1,0:T(2,128)S(1)}, u32[]{:S(2)}, u32[]{:S(2)}) collective-permute-start(f32[2,20,2,128]{3,2,1,0:T(2,128)S(1)} %get-tuple-element.45), channel_id=1, source_target_pairs={{0,1},{1,2},{2,3},{3,4},{4,5},{5,6},{6,7},{8,9},{9,10},{10,11},{11... | collective-permute-start | bytes 122888 | tf_op jit(solution)/shard_map/ppermute | solution.py:21
  162.4 16.7 %copy.517 = f32[2,16,32,128]{0,3,2,1:T(8,128)} copy(f32[2,16,32,128]{3,2,1,0:T(8,128)S(1)} %fusion.70) | data formatting | bytes 1048576 | tf_op jit(solution)/shard_map/div | solution.py:86
  179.1 3.0 gather_fusion.3
  182.3 2.0 fusion.58
  184.3 1.3 collective-permute-start.16
  185.6 4.9 collective-permute-start.17
  190.7 1.6 collective-permute-done.17
  193.7 7.1 %collective-permute-start.19 = (f32[2,20,2,128]{3,2,1,0:T(2,128)S(1)}, f32[2,20,2,128]{3,2,1,0:T(2,128)S(1)}, u32[]{:S(2)}, u32[]{:S(2)}) collective-permute-start(f32[2,20,2,128]{3,2,1,0:T(2,128)S(1)} %get-tuple-element.41), channel_id=1, source_target_pairs={{0,1},{1,2},{2,3},{3,4},{4,5},{5,6},{6,7},{8,9},{9,10},{10,11},{11... | collective-permute-start | bytes 122888 | tf_op jit(solution)/shard_map/ppermute | solution.py:21
  201.7 16.7 %copy.518 = f32[2,16,32,128]{0,3,2,1:T(8,128)} copy(f32[2,16,32,128]{3,2,1,0:T(8,128)S(1)} %fusion.58) | data formatting | bytes 1048576 | tf_op jit(solution)/shard_map/div | solution.py:86
  218.4 3.0 gather_fusion.4
  221.6 2.0 fusion.46
  224.9 4.9 collective-permute-start.21
  230.1 1.6 collective-permute-done.21
  233.0 6.9 %collective-permute-start.23 = (f32[2,20,2,128]{3,2,1,0:T(2,128)S(1)}, f32[2,20,2,128]{3,2,1,0:T(2,128)S(1)}, u32[]{:S(2)}, u32[]{:S(2)}) collective-permute-start(f32[2,20,2,128]{3,2,1,0:T(2,128)S(1)} %get-tuple-element.37), channel_id=1, source_target_pairs={{0,1},{1,2},{2,3},{3,4},{4,5},{5,6},{6,7},{8,9},{9,10},{10,11},{11... | collective-permute-start | bytes 122888 | tf_op jit(solution)/shard_map/ppermute | solution.py:21
  240.9 16.7 %copy.519 = f32[2,16,32,128]{0,3,2,1:T(8,128)} copy(f32[2,16,32,128]{3,2,1,0:T(8,128)S(1)} %fusion.46) | data formatting | bytes 1048576 | tf_op jit(solution)/shard_map/div | solution.py:86
  257.6 3.0 gather_fusion.5
  260.8 2.0 fusion.34
  264.1 4.9 collective-permute-start.25
  269.3 1.6 collective-permute-done.25
  272.2 6.9 %collective-permute-start.27 = (f32[2,20,2,128]{3,2,1,0:T(2,128)S(1)}, f32[2,20,2,128]{3,2,1,0:T(2,128)S(1)}, u32[]{:S(2)}, u32[]{:S(2)}) collective-permute-start(f32[2,20,2,128]{3,2,1,0:T(2,128)S(1)} %get-tuple-element.33), channel_id=1, source_target_pairs={{0,1},{1,2},{2,3},{3,4},{4,5},{5,6},{6,7},{8,9},{9,10},{10,11},{11... | collective-permute-start | bytes 122888 | tf_op jit(solution)/shard_map/ppermute | solution.py:21
  280.1 16.7 %copy.520 = f32[2,16,32,128]{0,3,2,1:T(8,128)} copy(f32[2,16,32,128]{3,2,1,0:T(8,128)S(1)} %fusion.34) | data formatting | bytes 1048576 | tf_op jit(solution)/shard_map/div | solution.py:86
  296.8 3.0 gather_fusion.6
  299.9 2.0 fusion.22
  303.2 4.9 collective-permute-start.29
  308.4 1.6 collective-permute-done.29
  311.3 7.2 %collective-permute-start.31 = (f32[2,20,2,128]{3,2,1,0:T(2,128)S(1)}, f32[2,20,2,128]{3,2,1,0:T(2,128)S(1)}, u32[]{:S(2)}, u32[]{:S(2)}) collective-permute-start(f32[2,20,2,128]{3,2,1,0:T(2,128)S(1)} %get-tuple-element.29), channel_id=1, source_target_pairs={{0,1},{1,2},{2,3},{3,4},{4,5},{5,6},{6,7},{8,9},{9,10},{10,11},{11... | collective-permute-start | bytes 122888 | tf_op jit(solution)/shard_map/ppermute | solution.py:21
  319.5 16.7 %copy.521 = f32[2,16,32,128]{0,3,2,1:T(8,128)} copy(f32[2,16,32,128]{3,2,1,0:T(8,128)S(1)} %fusion.22) | data formatting | bytes 1048576 | tf_op jit(solution)/shard_map/div | solution.py:86
  336.1 3.0 gather_fusion.7
  339.3 2.0 fusion.10
  341.3 16.8 %copy.522 = f32[2,16,32,128]{0,3,2,1:T(8,128)} copy(f32[2,16,32,128]{3,2,1,0:T(8,128)S(1)} %fusion.10) | data formatting | bytes 1048576 | tf_op jit(solution)/shard_map/div | solution.py:86
  358.1 2.4 gather_fusion.8
  360.5 1.4 bitcast_select_fusion
  362.6 183.4 %psum.7 = f32[1,2,256,8]{2,3,1,0:T(8,128)} all-reduce(f32[1,2,256,8]{2,3,1,0:T(8,128)S(1)} %bitcast.70), channel_id=1, replica_groups=mesh['shot'=4,'gx'=4,'gy'=8] {'gx','gy'}, use_global_device_ids=true, to_apply=%region_1.2 | all-reduce | flops 4096 | bytes 32768 | tf_op jit(solution)/shard_map/psum | solution.py:138
  (124 shorter events, 28.7 us)
Async XLA Ops:
  7.2 97.1 %copy-start.1 = (f32[1,2,16,32,128]{4,3,2,1,0:T(8,128)S(1)}, f32[1,2,16,32,128]{4,3,2,1,0:T(8,128)}, u32[]{:S(2)}) copy-start(f32[1,2,16,32,128]{4,3,2,1,0:T(8,128)} %param.11) | copy-start | bytes 1572868
  7.2 54.9 %all-gather.2.cloned.1.call-start = ((), (), s32[]{:S(2)}) async-start(), calls=%async_computation | async-start | bytes 4456448 | tf_op jit(solution)/shard_map/all_gather | solution.py:113
  8.8 17.0 %collective-permute-start = (f32[2,2,32,128]{3,2,1,0:T(8,128)S(1)}, f32[2,2,32,128]{3,2,1,0:T(8,128)S(1)}, u32[]{:S(2)}, u32[]{:S(2)}) collective-permute-start(f32[2,2,32,128]{3,2,1,0:T(8,128)S(1)} %get-tuple-element.104), channel_id=1, source_target_pairs={{8,0},{16,8},{24,16},{9,1},{17,9},{25,17},{10,2},{18,10},{26,18},{... | collective-permute-start | bytes 196616 | tf_op jit(solution)/shard_map/ppermute | solution.py:23
  10.1 15.8 %collective-permute-start.1 = (f32[2,2,32,128]{3,2,1,0:T(8,128)S(1)}, f32[2,2,32,128]{3,2,1,0:T(8,128)S(1)}, u32[]{:S(2)}, u32[]{:S(2)}) collective-permute-start(f32[2,2,32,128]{3,2,1,0:T(8,128)S(1)} %get-tuple-element.105), channel_id=1, source_target_pairs={{0,8},{8,16},{16,24},{1,9},{9,17},{17,25},{2,10},{10,18},{18,26},{... | collective-permute-start | bytes 196616 | tf_op jit(solution)/shard_map/ppermute | solution.py:21
  25.8 39.0 %copy-start.3 = (f32[2,2,32,128]{3,2,1,0:T(8,128)}, f32[2,2,32,128]{3,2,1,0:T(8,128)S(1)}, u32[]{:S(2)}) copy-start(f32[2,2,32,128]{3,2,1,0:T(8,128)S(1)} %collective-permute-done) | copy-start | bytes 196612
  25.9 39.0 %copy-start.4 = (f32[2,2,32,128]{3,2,1,0:T(8,128)}, f32[2,2,32,128]{3,2,1,0:T(8,128)S(1)}, u32[]{:S(2)}) copy-start(f32[2,2,32,128]{3,2,1,0:T(8,128)S(1)} %collective-permute-done.1) | copy-start | bytes 196612
  26.9 7.7 %collective-permute-start.2 = (f32[2,20,2,128]{3,2,1,0:T(2,128)S(1)}, f32[2,20,2,128]{3,2,1,0:T(2,128)S(1)}, u32[]{:S(2)}, u32[]{:S(2)}) collective-permute-start(f32[2,20,2,128]{3,2,1,0:T(2,128)S(1)} %get-tuple-element.56), channel_id=1, source_target_pairs={{1,0},{2,1},{3,2},{4,3},{5,4},{6,5},{7,6},{9,8},{10,9},{11,10},{12... | collective-permute-start | bytes 122888 | tf_op jit(solution)/shard_map/ppermute | solution.py:23
  28.2 7.9 %collective-permute-start.3 = (f32[2,20,2,128]{3,2,1,0:T(2,128)S(1)}, f32[2,20,2,128]{3,2,1,0:T(2,128)S(1)}, u32[]{:S(2)}, u32[]{:S(2)}) collective-permute-start(f32[2,20,2,128]{3,2,1,0:T(2,128)S(1)} %get-tuple-element.57), channel_id=1, source_target_pairs={{0,1},{1,2},{2,3},{3,4},{4,5},{5,6},{6,7},{8,9},{9,10},{10,11},{11... | collective-permute-start | bytes 122888 | tf_op jit(solution)/shard_map/ppermute | solution.py:21
  68.1 6.8 %collective-permute-start.4 = (f32[2,2,32,128]{3,2,1,0:T(8,128)S(1)}, f32[2,2,32,128]{3,2,1,0:T(8,128)S(1)}, u32[]{:S(2)}, u32[]{:S(2)}) collective-permute-start(f32[2,2,32,128]{3,2,1,0:T(8,128)S(1)} %get-tuple-element.98), channel_id=1, source_target_pairs={{8,0},{16,8},{24,16},{9,1},{17,9},{25,17},{10,2},{18,10},{26,18},{... | collective-permute-start | bytes 196616 | tf_op jit(solution)/shard_map/ppermute | solution.py:23
  69.4 6.7 %collective-permute-start.5 = (f32[2,2,32,128]{3,2,1,0:T(8,128)S(1)}, f32[2,2,32,128]{3,2,1,0:T(8,128)S(1)}, u32[]{:S(2)}, u32[]{:S(2)}) collective-permute-start(f32[2,2,32,128]{3,2,1,0:T(8,128)S(1)} %get-tuple-element.99), channel_id=1, source_target_pairs={{0,8},{8,16},{16,24},{1,9},{9,17},{17,25},{2,10},{10,18},{18,26},{... | collective-permute-start | bytes 196616 | tf_op jit(solution)/shard_map/ppermute | solution.py:21
  76.0 28.2 %copy-start.11 = (f32[2,2,32,128]{3,2,1,0:T(8,128)}, f32[2,2,32,128]{3,2,1,0:T(8,128)S(1)}, u32[]{:S(2)}) copy-start(f32[2,2,32,128]{3,2,1,0:T(8,128)S(1)} %collective-permute-done.5) | copy-start | bytes 196612
  76.1 28.0 %collective-permute-start.6 = (f32[2,20,2,128]{3,2,1,0:T(2,128)S(1)}, f32[2,20,2,128]{3,2,1,0:T(2,128)S(1)}, u32[]{:S(2)}, u32[]{:S(2)}) collective-permute-start(f32[2,20,2,128]{3,2,1,0:T(2,128)S(1)} %get-tuple-element.52), channel_id=1, source_target_pairs={{1,0},{2,1},{3,2},{4,3},{5,4},{6,5},{7,6},{9,8},{10,9},{11,10},{12... | collective-permute-start | bytes 122888 | tf_op jit(solution)/shard_map/ppermute | solution.py:23
  77.4 26.7 %collective-permute-start.7 = (f32[2,20,2,128]{3,2,1,0:T(2,128)S(1)}, f32[2,20,2,128]{3,2,1,0:T(2,128)S(1)}, u32[]{:S(2)}, u32[]{:S(2)}) collective-permute-start(f32[2,20,2,128]{3,2,1,0:T(2,128)S(1)} %get-tuple-element.53), channel_id=1, source_target_pairs={{0,1},{1,2},{2,3},{3,4},{4,5},{5,6},{6,7},{8,9},{9,10},{10,11},{11... | collective-permute-start | bytes 122888 | tf_op jit(solution)/shard_map/ppermute | solution.py:21
  106.2 6.6 %collective-permute-start.8 = (f32[2,2,32,128]{3,2,1,0:T(8,128)S(1)}, f32[2,2,32,128]{3,2,1,0:T(8,128)S(1)}, u32[]{:S(2)}, u32[]{:S(2)}) collective-permute-start(f32[2,2,32,128]{3,2,1,0:T(8,128)S(1)} %get-tuple-element.92), channel_id=1, source_target_pairs={{8,0},{16,8},{24,16},{9,1},{17,9},{25,17},{10,2},{18,10},{26,18},{... | collective-permute-start | bytes 196616 | tf_op jit(solution)/shard_map/ppermute | solution.py:23
  107.5 6.9 %collective-permute-start.9 = (f32[2,2,32,128]{3,2,1,0:T(8,128)S(1)}, f32[2,2,32,128]{3,2,1,0:T(8,128)S(1)}, u32[]{:S(2)}, u32[]{:S(2)}) collective-permute-start(f32[2,2,32,128]{3,2,1,0:T(8,128)S(1)} %get-tuple-element.93), channel_id=1, source_target_pairs={{0,8},{8,16},{16,24},{1,9},{9,17},{17,25},{2,10},{10,18},{18,26},{... | collective-permute-start | bytes 196616 | tf_op jit(solution)/shard_map/ppermute | solution.py:21
  114.4 28.7 %copy-start.6 = (f32[2,2,32,128]{3,2,1,0:T(8,128)}, f32[2,2,32,128]{3,2,1,0:T(8,128)S(1)}, u32[]{:S(2)}) copy-start(f32[2,2,32,128]{3,2,1,0:T(8,128)S(1)} %collective-permute-done.9) | copy-start | bytes 196612
  114.5 28.5 %collective-permute-start.10 = (f32[2,20,2,128]{3,2,1,0:T(2,128)S(1)}, f32[2,20,2,128]{3,2,1,0:T(2,128)S(1)}, u32[]{:S(2)}, u32[]{:S(2)}) collective-permute-start(f32[2,20,2,128]{3,2,1,0:T(2,128)S(1)} %get-tuple-element.48), channel_id=1, source_target_pairs={{1,0},{2,1},{3,2},{4,3},{5,4},{6,5},{7,6},{9,8},{10,9},{11,10},{12... | collective-permute-start | bytes 122888 | tf_op jit(solution)/shard_map/ppermute | solution.py:23
  115.8 27.2 %collective-permute-start.11 = (f32[2,20,2,128]{3,2,1,0:T(2,128)S(1)}, f32[2,20,2,128]{3,2,1,0:T(2,128)S(1)}, u32[]{:S(2)}, u32[]{:S(2)}) collective-permute-start(f32[2,20,2,128]{3,2,1,0:T(2,128)S(1)} %get-tuple-element.49), channel_id=1, source_target_pairs={{0,1},{1,2},{2,3},{3,4},{4,5},{5,6},{6,7},{8,9},{9,10},{10,11},{11... | collective-permute-start | bytes 122888 | tf_op jit(solution)/shard_map/ppermute | solution.py:21
  145.1 6.5 %collective-permute-start.12 = (f32[2,2,32,128]{3,2,1,0:T(8,128)S(1)}, f32[2,2,32,128]{3,2,1,0:T(8,128)S(1)}, u32[]{:S(2)}, u32[]{:S(2)}) collective-permute-start(f32[2,2,32,128]{3,2,1,0:T(8,128)S(1)} %get-tuple-element.86), channel_id=1, source_target_pairs={{8,0},{16,8},{24,16},{9,1},{17,9},{25,17},{10,2},{18,10},{26,18},{... | collective-permute-start | bytes 196616 | tf_op jit(solution)/shard_map/ppermute | solution.py:23
  146.4 6.8 %collective-permute-start.13 = (f32[2,2,32,128]{3,2,1,0:T(8,128)S(1)}, f32[2,2,32,128]{3,2,1,0:T(8,128)S(1)}, u32[]{:S(2)}, u32[]{:S(2)}) collective-permute-start(f32[2,2,32,128]{3,2,1,0:T(8,128)S(1)} %get-tuple-element.87), channel_id=1, source_target_pairs={{0,8},{8,16},{16,24},{1,9},{9,17},{17,25},{2,10},{10,18},{18,26},{... | collective-permute-start | bytes 196616 | tf_op jit(solution)/shard_map/ppermute | solution.py:21
  153.2 29.1 %copy-start.7 = (f32[2,2,32,128]{3,2,1,0:T(8,128)}, f32[2,2,32,128]{3,2,1,0:T(8,128)S(1)}, u32[]{:S(2)}) copy-start(f32[2,2,32,128]{3,2,1,0:T(8,128)S(1)} %collective-permute-done.13) | copy-start | bytes 196612
  153.2 28.9 %collective-permute-start.14 = (f32[2,20,2,128]{3,2,1,0:T(2,128)S(1)}, f32[2,20,2,128]{3,2,1,0:T(2,128)S(1)}, u32[]{:S(2)}, u32[]{:S(2)}) collective-permute-start(f32[2,20,2,128]{3,2,1,0:T(2,128)S(1)} %get-tuple-element.44), channel_id=1, source_target_pairs={{1,0},{2,1},{3,2},{4,3},{5,4},{6,5},{7,6},{9,8},{10,9},{11,10},{12... | collective-permute-start | bytes 122888 | tf_op jit(solution)/shard_map/ppermute | solution.py:23
  154.5 27.6 %collective-permute-start.15 = (f32[2,20,2,128]{3,2,1,0:T(2,128)S(1)}, f32[2,20,2,128]{3,2,1,0:T(2,128)S(1)}, u32[]{:S(2)}, u32[]{:S(2)}) collective-permute-start(f32[2,20,2,128]{3,2,1,0:T(2,128)S(1)} %get-tuple-element.45), channel_id=1, source_target_pairs={{0,1},{1,2},{2,3},{3,4},{4,5},{5,6},{6,7},{8,9},{9,10},{10,11},{11... | collective-permute-start | bytes 122888 | tf_op jit(solution)/shard_map/ppermute | solution.py:21
  184.3 6.5 %collective-permute-start.16 = (f32[2,2,32,128]{3,2,1,0:T(8,128)S(1)}, f32[2,2,32,128]{3,2,1,0:T(8,128)S(1)}, u32[]{:S(2)}, u32[]{:S(2)}) collective-permute-start(f32[2,2,32,128]{3,2,1,0:T(8,128)S(1)} %get-tuple-element.80), channel_id=1, source_target_pairs={{8,0},{16,8},{24,16},{9,1},{17,9},{25,17},{10,2},{18,10},{26,18},{... | collective-permute-start | bytes 196616 | tf_op jit(solution)/shard_map/ppermute | solution.py:23
  185.6 6.8 %collective-permute-start.17 = (f32[2,2,32,128]{3,2,1,0:T(8,128)S(1)}, f32[2,2,32,128]{3,2,1,0:T(8,128)S(1)}, u32[]{:S(2)}, u32[]{:S(2)}) collective-permute-start(f32[2,2,32,128]{3,2,1,0:T(8,128)S(1)} %get-tuple-element.81), channel_id=1, source_target_pairs={{0,8},{8,16},{16,24},{1,9},{9,17},{17,25},{2,10},{10,18},{18,26},{... | collective-permute-start | bytes 196616 | tf_op jit(solution)/shard_map/ppermute | solution.py:21
  192.3 29.3 %copy-start.8 = (f32[2,2,32,128]{3,2,1,0:T(8,128)}, f32[2,2,32,128]{3,2,1,0:T(8,128)S(1)}, u32[]{:S(2)}) copy-start(f32[2,2,32,128]{3,2,1,0:T(8,128)S(1)} %collective-permute-done.17) | copy-start | bytes 196612
  192.4 29.1 %collective-permute-start.18 = (f32[2,20,2,128]{3,2,1,0:T(2,128)S(1)}, f32[2,20,2,128]{3,2,1,0:T(2,128)S(1)}, u32[]{:S(2)}, u32[]{:S(2)}) collective-permute-start(f32[2,20,2,128]{3,2,1,0:T(2,128)S(1)} %get-tuple-element.40), channel_id=1, source_target_pairs={{1,0},{2,1},{3,2},{4,3},{5,4},{6,5},{7,6},{9,8},{10,9},{11,10},{12... | collective-permute-start | bytes 122888 | tf_op jit(solution)/shard_map/ppermute | solution.py:23
  193.7 27.8 %collective-permute-start.19 = (f32[2,20,2,128]{3,2,1,0:T(2,128)S(1)}, f32[2,20,2,128]{3,2,1,0:T(2,128)S(1)}, u32[]{:S(2)}, u32[]{:S(2)}) collective-permute-start(f32[2,20,2,128]{3,2,1,0:T(2,128)S(1)} %get-tuple-element.41), channel_id=1, source_target_pairs={{0,1},{1,2},{2,3},{3,4},{4,5},{5,6},{6,7},{8,9},{9,10},{10,11},{11... | collective-permute-start | bytes 122888 | tf_op jit(solution)/shard_map/ppermute | solution.py:21
  223.6 6.5 %collective-permute-start.20 = (f32[2,2,32,128]{3,2,1,0:T(8,128)S(1)}, f32[2,2,32,128]{3,2,1,0:T(8,128)S(1)}, u32[]{:S(2)}, u32[]{:S(2)}) collective-permute-start(f32[2,2,32,128]{3,2,1,0:T(8,128)S(1)} %get-tuple-element.74), channel_id=1, source_target_pairs={{8,0},{16,8},{24,16},{9,1},{17,9},{25,17},{10,2},{18,10},{26,18},{... | collective-permute-start | bytes 196616 | tf_op jit(solution)/shard_map/ppermute | solution.py:23
  224.9 6.8 %collective-permute-start.21 = (f32[2,2,32,128]{3,2,1,0:T(8,128)S(1)}, f32[2,2,32,128]{3,2,1,0:T(8,128)S(1)}, u32[]{:S(2)}, u32[]{:S(2)}) collective-permute-start(f32[2,2,32,128]{3,2,1,0:T(8,128)S(1)} %get-tuple-element.75), channel_id=1, source_target_pairs={{0,8},{8,16},{16,24},{1,9},{9,17},{17,25},{2,10},{10,18},{18,26},{... | collective-permute-start | bytes 196616 | tf_op jit(solution)/shard_map/ppermute | solution.py:21
  231.7 29.1 %copy-start.9 = (f32[2,2,32,128]{3,2,1,0:T(8,128)}, f32[2,2,32,128]{3,2,1,0:T(8,128)S(1)}, u32[]{:S(2)}) copy-start(f32[2,2,32,128]{3,2,1,0:T(8,128)S(1)} %collective-permute-done.21) | copy-start | bytes 196612
  231.7 28.9 %collective-permute-start.22 = (f32[2,20,2,128]{3,2,1,0:T(2,128)S(1)}, f32[2,20,2,128]{3,2,1,0:T(2,128)S(1)}, u32[]{:S(2)}, u32[]{:S(2)}) collective-permute-start(f32[2,20,2,128]{3,2,1,0:T(2,128)S(1)} %get-tuple-element.36), channel_id=1, source_target_pairs={{1,0},{2,1},{3,2},{4,3},{5,4},{6,5},{7,6},{9,8},{10,9},{11,10},{12... | collective-permute-start | bytes 122888 | tf_op jit(solution)/shard_map/ppermute | solution.py:23
  233.0 27.6 %collective-permute-start.23 = (f32[2,20,2,128]{3,2,1,0:T(2,128)S(1)}, f32[2,20,2,128]{3,2,1,0:T(2,128)S(1)}, u32[]{:S(2)}, u32[]{:S(2)}) collective-permute-start(f32[2,20,2,128]{3,2,1,0:T(2,128)S(1)} %get-tuple-element.37), channel_id=1, source_target_pairs={{0,1},{1,2},{2,3},{3,4},{4,5},{5,6},{6,7},{8,9},{9,10},{10,11},{11... | collective-permute-start | bytes 122888 | tf_op jit(solution)/shard_map/ppermute | solution.py:21
  262.8 6.5 %collective-permute-start.24 = (f32[2,2,32,128]{3,2,1,0:T(8,128)S(1)}, f32[2,2,32,128]{3,2,1,0:T(8,128)S(1)}, u32[]{:S(2)}, u32[]{:S(2)}) collective-permute-start(f32[2,2,32,128]{3,2,1,0:T(8,128)S(1)} %get-tuple-element.68), channel_id=1, source_target_pairs={{8,0},{16,8},{24,16},{9,1},{17,9},{25,17},{10,2},{18,10},{26,18},{... | collective-permute-start | bytes 196616 | tf_op jit(solution)/shard_map/ppermute | solution.py:23
  264.1 6.8 %collective-permute-start.25 = (f32[2,2,32,128]{3,2,1,0:T(8,128)S(1)}, f32[2,2,32,128]{3,2,1,0:T(8,128)S(1)}, u32[]{:S(2)}, u32[]{:S(2)}) collective-permute-start(f32[2,2,32,128]{3,2,1,0:T(8,128)S(1)} %get-tuple-element.69), channel_id=1, source_target_pairs={{0,8},{8,16},{16,24},{1,9},{9,17},{17,25},{2,10},{10,18},{18,26},{... | collective-permute-start | bytes 196616 | tf_op jit(solution)/shard_map/ppermute | solution.py:21
  270.8 29.1 %copy-start.10 = (f32[2,2,32,128]{3,2,1,0:T(8,128)}, f32[2,2,32,128]{3,2,1,0:T(8,128)S(1)}, u32[]{:S(2)}) copy-start(f32[2,2,32,128]{3,2,1,0:T(8,128)S(1)} %collective-permute-done.25) | copy-start | bytes 196612
  270.9 28.9 %collective-permute-start.26 = (f32[2,20,2,128]{3,2,1,0:T(2,128)S(1)}, f32[2,20,2,128]{3,2,1,0:T(2,128)S(1)}, u32[]{:S(2)}, u32[]{:S(2)}) collective-permute-start(f32[2,20,2,128]{3,2,1,0:T(2,128)S(1)} %get-tuple-element.32), channel_id=1, source_target_pairs={{1,0},{2,1},{3,2},{4,3},{5,4},{6,5},{7,6},{9,8},{10,9},{11,10},{12... | collective-permute-start | bytes 122888 | tf_op jit(solution)/shard_map/ppermute | solution.py:23
  272.2 27.6 %collective-permute-start.27 = (f32[2,20,2,128]{3,2,1,0:T(2,128)S(1)}, f32[2,20,2,128]{3,2,1,0:T(2,128)S(1)}, u32[]{:S(2)}, u32[]{:S(2)}) collective-permute-start(f32[2,20,2,128]{3,2,1,0:T(2,128)S(1)} %get-tuple-element.33), channel_id=1, source_target_pairs={{0,1},{1,2},{2,3},{3,4},{4,5},{5,6},{6,7},{8,9},{9,10},{10,11},{11... | collective-permute-start | bytes 122888 | tf_op jit(solution)/shard_map/ppermute | solution.py:21
  301.9 56.2 %copy-start = (f32[2,16,32,128]{3,2,1,0:T(8,128)}, f32[2,16,32,128]{3,2,1,0:T(8,128)S(1)}, u32[]{:S(2)}) copy-start(f32[2,16,32,128]{3,2,1,0:T(8,128)S(1)} %fusion.22) | copy-start | bytes 1572868
  301.9 6.5 %collective-permute-start.28 = (f32[2,2,32,128]{3,2,1,0:T(8,128)S(1)}, f32[2,2,32,128]{3,2,1,0:T(8,128)S(1)}, u32[]{:S(2)}, u32[]{:S(2)}) collective-permute-start(f32[2,2,32,128]{3,2,1,0:T(8,128)S(1)} %get-tuple-element.62), channel_id=1, source_target_pairs={{8,0},{16,8},{24,16},{9,1},{17,9},{25,17},{10,2},{18,10},{26,18},{... | collective-permute-start | bytes 196616 | tf_op jit(solution)/shard_map/ppermute | solution.py:23
  303.2 6.8 %collective-permute-start.29 = (f32[2,2,32,128]{3,2,1,0:T(8,128)S(1)}, f32[2,2,32,128]{3,2,1,0:T(8,128)S(1)}, u32[]{:S(2)}, u32[]{:S(2)}) collective-permute-start(f32[2,2,32,128]{3,2,1,0:T(8,128)S(1)} %get-tuple-element.63), channel_id=1, source_target_pairs={{0,8},{8,16},{16,24},{1,9},{9,17},{17,25},{2,10},{10,18},{18,26},{... | collective-permute-start | bytes 196616 | tf_op jit(solution)/shard_map/ppermute | solution.py:21
  310.0 29.3 %copy-start.5 = (f32[2,2,32,128]{3,2,1,0:T(8,128)}, f32[2,2,32,128]{3,2,1,0:T(8,128)S(1)}, u32[]{:S(2)}) copy-start(f32[2,2,32,128]{3,2,1,0:T(8,128)S(1)} %collective-permute-done.29) | copy-start | bytes 196612
  310.0 29.1 %collective-permute-start.30 = (f32[2,20,2,128]{3,2,1,0:T(2,128)S(1)}, f32[2,20,2,128]{3,2,1,0:T(2,128)S(1)}, u32[]{:S(2)}, u32[]{:S(2)}) collective-permute-start(f32[2,20,2,128]{3,2,1,0:T(2,128)S(1)} %get-tuple-element.28), channel_id=1, source_target_pairs={{1,0},{2,1},{3,2},{4,3},{5,4},{6,5},{7,6},{9,8},{10,9},{11,10},{12... | collective-permute-start | bytes 122888 | tf_op jit(solution)/shard_map/ppermute | solution.py:23
  311.3 27.8 %collective-permute-start.31 = (f32[2,20,2,128]{3,2,1,0:T(2,128)S(1)}, f32[2,20,2,128]{3,2,1,0:T(2,128)S(1)}, u32[]{:S(2)}, u32[]{:S(2)}) collective-permute-start(f32[2,20,2,128]{3,2,1,0:T(2,128)S(1)} %get-tuple-element.29), channel_id=1, source_target_pairs={{0,1},{1,2},{2,3},{3,4},{4,5},{5,6},{6,7},{8,9},{9,10},{10,11},{11... | collective-permute-start | bytes 122888 | tf_op jit(solution)/shard_map/ppermute | solution.py:21
  341.3 204.7 %copy-start.2 = (f32[2,16,32,128]{3,2,1,0:T(8,128)}, f32[2,16,32,128]{3,2,1,0:T(8,128)S(1)}, u32[]{:S(2)}) copy-start(f32[2,16,32,128]{3,2,1,0:T(8,128)S(1)} %fusion.10) | copy-start | bytes 1572868
  341.3 19.2 %copy-start.12 = (f32[256,2]{1,0:T(8,128)S(1)}, f32[256,2]{1,0:T(8,128)}, u32[]{:S(2)}) copy-start(f32[256,2]{1,0:T(8,128)} %gather_fusion.7) | copy-start | bytes 6148
Sparse Core Ops, SparseCore 0:
  9.7 52.3 all-gather.1
where the time goes:
time: 554 us; the launch traced here: 553 us
  blocking collectives  183 us (33%)
  local copies, waits for them, and re-layouts  177 us (32%)
  starting transfers between devices  113 us (20%)
  waiting for transfers between devices  39.1 us (7%)
  other arithmetic  24.3 us (4%)
  between operations  16 us (3%)
    psum x1, blocking collectives, local(): traces = lax.psum(jnp.stack(recorded, axis=-1), ('gx', 'gy'))  183 us
    div x8, local copies, waits for them, and re-layouts, advance(): (2.0 * middle - (1.0 - damp) * previous + coef * laplace(extended) + inje...  134 us
    ppermute x16, starting transfers between devices, extended_2(): lax.ppermute(tail, axis, [(i, (i + 1) % count) for i in range(ends)])  92.2 us
    all_gather x1, waiting for transfers between devices, local(): piece = lax.all_gather(model_tiles, ('shot', 'gx'), axis=0, tiled=True)  24.6 us
    gather x8, local copies, waits for them, and re-layouts, sample(): field[:, jnp.clip(local_x, 0, size_x - 1), jnp.clip(local_y, 0, size_y -...  23.6 us
    ppermute x16, starting transfers between devices, extended_2(): lax.ppermute(head, axis, [((i + 1) % count, i) for i in range(ends)])  20.7 us
    div x8, other arithmetic, advance(): (2.0 * middle - (1.0 - damp) * previous + coef * laplace(extended) + inje...  16.9 us
    slice x16, local copies, waits for them, and re-layouts, depth_ahead(): return jnp.concatenate([field[..., reach:], filler], axis=-1)  12.5 us
  transfers between devices with their start and end apart: 33, of which 17 were waited for; matrix products, arithmetic and copies ran while one was open for 29% of the time, Pallas kernels for 0%

commit v1 on v0

--- a/solution.py
+++ b/solution.py
@@ -8,6 +8,12 @@
 near_weight = 4.0 / 3.0
 far_weight = -1.0 / 12.0
 damp_peak = 0.3
+
+
+def gather_and_add(shard, mesh_axis):
+    pieces = lax.all_gather(shard, mesh_axis, axis=0, tiled=False)
+    summed = pieces.sum(axis=0)
+    return summed
 
 
 def extended_2(cells, sides, width):
@@ -135,7 +141,7 @@
         recorded.append(sample(fresh, receiver_cells, x_start, y_start))
         previous = current
         current = fresh
-    traces = lax.psum(jnp.stack(recorded, axis=-1), ("gx", "gy"))
+    traces = gather_and_add(jnp.stack(recorded, axis=-1), ("gx", "gy"))
     return (current[None], previous[None], traces[None])
 
 

time: 554 us -> 469 us (0.85)
  blocking collectives: 183 us -> 97.4 us
    psum x1 -> x0, blocking collectives: 183 us -> none  [local(): traces = lax.psum(jnp.stack(recorded, axis=-1), ('gx', 'gy'))]
    all_gather x0 -> x1, blocking collectives: none -> 97.4 us  [gather_and_add(): pieces = lax.all_gather(shard, mesh_axis, axis=0, tiled=False)]
  transfers between devices with their start and end apart: 33 -> 33, of which waited for: 17 -> 17; matrix products, arithmetic and copies ran while one was open for 29% -> 34% of each run, Pallas kernels for 0% -> 0%
where the time goes in v1:
time: 469 us; the launch traced here: 468 us
  local copies, waits for them, and re-layouts  177 us (38%)
  starting transfers between devices  113 us (24%)
  blocking collectives  97.4 us (21%)
  waiting for transfers between devices  39.1 us (8%)
  other arithmetic  24.9 us (5%)
  between operations  16 us (3%)
    div x8, local copies, waits for them, and re-layouts, advance(): (2.0 * middle - (1.0 - damp) * previous + coef * laplace(extended) + inje...  134 us
    all_gather x1, blocking collectives, gather_and_add(): pieces = lax.all_gather(shard, mesh_axis, axis=0, tiled=False)  97.4 us
    ppermute x16, starting transfers between devices, extended_2(): lax.ppermute(tail, axis, [(i, (i + 1) % count) for i in range(ends)])  92.2 us
    all_gather x1, waiting for transfers between devices, local(): piece = lax.all_gather(model_tiles, ('shot', 'gx'), axis=0, tiled=True)  24.6 us
    gather x8, local copies, waits for them, and re-layouts, sample(): field[:, jnp.clip(local_x, 0, size_x - 1), jnp.clip(local_y, 0, size_y -...  23.6 us
    ppermute x16, starting transfers between devices, extended_2(): lax.ppermute(head, axis, [((i + 1) % count, i) for i in range(ends)])  20.7 us
    div x8, other arithmetic, advance(): (2.0 * middle - (1.0 - damp) * previous + coef * laplace(extended) + inje...  16.9 us
    slice x16, local copies, waits for them, and re-layouts, depth_ahead(): return jnp.concatenate([field[..., reach:], filler], axis=-1)  12.5 us
  transfers between devices with their start and end apart: 33, of which 17 were waited for; matrix products, arithmetic and copies ran while one was open for 34% of the time, Pallas kernels for 0%

profile of v1, /device:TPU:0, one launch (start us, length us, event | category | flops | bytes accessed | tf_op | source)
XLA Modules:
  0.0 467.5 jit_solution(7927539147912254033)
XLA Ops:
  8.8 1.3 collective-permute-start
  10.1 4.5 collective-permute-start.1
  15.3 1.3 fusion.155
  21.3 2.2 fusion.179
  23.5 2.3 fusion.178
  26.9 1.3 collective-permute-start.2
  28.2 6.1 %collective-permute-start.3 = (f32[2,20,2,128]{3,2,1,0:T(2,128)S(1)}, f32[2,20,2,128]{3,2,1,0:T(2,128)S(1)}, u32[]{:S(2)}, u32[]{:S(2)}) collective-permute-start(f32[2,20,2,128]{3,2,1,0:T(2,128)S(1)} %get-tuple-element.57), channel_id=1, source_target_pairs={{0,1},{1,2},{2,3},{3,4},{4,5},{5,6},{6,7},{8,9},{9,10},{10,11},{11... | collective-permute-start | bytes 122888 | tf_op jit(solution)/shard_map/ppermute | solution.py:27
  34.7 1.5 collective-permute-done.3
  36.1 1.4 pad_maximum_fusion
  37.5 24.6 %all-gather.3.cloned.1.call-done = f32[256,32,128]{2,1,0:T(8,128)} async-done(((f32[16,32,128]{2,1,0:T(8,128)}), f32[256,32,128]{2,1,0:T(8,128)}) %all-gather.3.cloned.1.call-update) | async-done | bytes 4194320 | tf_op jit(solution)/shard_map/all_gather | solution.py:119
  62.1 2.7 gather_fusion
  65.0 3.1 fusion.94
  68.1 1.3 collective-permute-start.4
  69.4 4.5 collective-permute-start.5
  76.1 1.3 collective-permute-start.6
  77.4 6.1 %collective-permute-start.7 = (f32[2,20,2,128]{3,2,1,0:T(2,128)S(1)}, f32[2,20,2,128]{3,2,1,0:T(2,128)S(1)}, u32[]{:S(2)}, u32[]{:S(2)}) collective-permute-start(f32[2,20,2,128]{3,2,1,0:T(2,128)S(1)} %get-tuple-element.53), channel_id=1, source_target_pairs={{0,1},{1,2},{2,3},{3,4},{4,5},{5,6},{6,7},{8,9},{9,10},{10,11},{11... | collective-permute-start | bytes 122888 | tf_op jit(solution)/shard_map/ppermute | solution.py:27
  84.4 16.7 %copy.514 = f32[2,16,32,128]{0,3,2,1:T(8,128)} copy(f32[2,16,32,128]{3,2,1,0:T(8,128)S(1)} %fusion.94) | data formatting | bytes 1048576 | tf_op jit(solution)/shard_map/div | solution.py:92
  101.0 3.0 gather_fusion.1
  104.2 2.0 fusion.82
  106.2 1.3 collective-permute-start.8
  107.5 5.0 %collective-permute-start.9 = (f32[2,2,32,128]{3,2,1,0:T(8,128)S(1)}, f32[2,2,32,128]{3,2,1,0:T(8,128)S(1)}, u32[]{:S(2)}, u32[]{:S(2)}) collective-permute-start(f32[2,2,32,128]{3,2,1,0:T(8,128)S(1)} %get-tuple-element.93), channel_id=1, source_target_pairs={{0,8},{8,16},{16,24},{1,9},{9,17},{17,25},{2,10},{10,18},{18,26},{... | collective-permute-start | bytes 196616 | tf_op jit(solution)/shard_map/ppermute | solution.py:27
  112.8 1.6 collective-permute-done.9
  114.5 1.3 collective-permute-start.10
  115.8 6.5 %collective-permute-start.11 = (f32[2,20,2,128]{3,2,1,0:T(2,128)S(1)}, f32[2,20,2,128]{3,2,1,0:T(2,128)S(1)}, u32[]{:S(2)}, u32[]{:S(2)}) collective-permute-start(f32[2,20,2,128]{3,2,1,0:T(2,128)S(1)} %get-tuple-element.49), channel_id=1, source_target_pairs={{0,1},{1,2},{2,3},{3,4},{4,5},{5,6},{6,7},{8,9},{9,10},{10,11},{11... | collective-permute-start | bytes 122888 | tf_op jit(solution)/shard_map/ppermute | solution.py:27
  123.2 16.7 %copy.515 = f32[2,16,32,128]{0,3,2,1:T(8,128)} copy(f32[2,16,32,128]{3,2,1,0:T(8,128)S(1)} %fusion.82) | data formatting | bytes 1048576 | tf_op jit(solution)/shard_map/div | solution.py:92
  139.9 3.0 gather_fusion.2
  143.1 2.0 fusion.70
  145.1 1.3 collective-permute-start.12
  146.4 4.9 %collective-permute-start.13 = (f32[2,2,32,128]{3,2,1,0:T(8,128)S(1)}, f32[2,2,32,128]{3,2,1,0:T(8,128)S(1)}, u32[]{:S(2)}, u32[]{:S(2)}) collective-permute-start(f32[2,2,32,128]{3,2,1,0:T(8,128)S(1)} %get-tuple-element.87), channel_id=1, source_target_pairs={{0,8},{8,16},{16,24},{1,9},{9,17},{17,25},{2,10},{10,18},{18,26},{... | collective-permute-start | bytes 196616 | tf_op jit(solution)/shard_map/ppermute | solution.py:27
  151.6 1.6 collective-permute-done.13
  153.2 1.3 collective-permute-start.14
  154.5 6.9 %collective-permute-start.15 = (f32[2,20,2,128]{3,2,1,0:T(2,128)S(1)}, f32[2,20,2,128]{3,2,1,0:T(2,128)S(1)}, u32[]{:S(2)}, u32[]{:S(2)}) collective-permute-start(f32[2,20,2,128]{3,2,1,0:T(2,128)S(1)} %get-tuple-element.45), channel_id=1, source_target_pairs={{0,1},{1,2},{2,3},{3,4},{4,5},{5,6},{6,7},{8,9},{9,10},{10,11},{11... | collective-permute-start | bytes 122888 | tf_op jit(solution)/shard_map/ppermute | solution.py:27
  162.4 16.7 %copy.516 = f32[2,16,32,128]{0,3,2,1:T(8,128)} copy(f32[2,16,32,128]{3,2,1,0:T(8,128)S(1)} %fusion.70) | data formatting | bytes 1048576 | tf_op jit(solution)/shard_map/div | solution.py:92
  179.1 3.0 gather_fusion.3
  182.3 2.0 fusion.58
  184.3 1.3 collective-permute-start.16
  185.6 4.9 %collective-permute-start.17 = (f32[2,2,32,128]{3,2,1,0:T(8,128)S(1)}, f32[2,2,32,128]{3,2,1,0:T(8,128)S(1)}, u32[]{:S(2)}, u32[]{:S(2)}) collective-permute-start(f32[2,2,32,128]{3,2,1,0:T(8,128)S(1)} %get-tuple-element.81), channel_id=1, source_target_pairs={{0,8},{8,16},{16,24},{1,9},{9,17},{17,25},{2,10},{10,18},{18,26},{... | collective-permute-start | bytes 196616 | tf_op jit(solution)/shard_map/ppermute | solution.py:27
  190.7 1.6 collective-permute-done.17
  193.7 7.1 %collective-permute-start.19 = (f32[2,20,2,128]{3,2,1,0:T(2,128)S(1)}, f32[2,20,2,128]{3,2,1,0:T(2,128)S(1)}, u32[]{:S(2)}, u32[]{:S(2)}) collective-permute-start(f32[2,20,2,128]{3,2,1,0:T(2,128)S(1)} %get-tuple-element.41), channel_id=1, source_target_pairs={{0,1},{1,2},{2,3},{3,4},{4,5},{5,6},{6,7},{8,9},{9,10},{10,11},{11... | collective-permute-start | bytes 122888 | tf_op jit(solution)/shard_map/ppermute | solution.py:27
  201.7 16.7 %copy.517 = f32[2,16,32,128]{0,3,2,1:T(8,128)} copy(f32[2,16,32,128]{3,2,1,0:T(8,128)S(1)} %fusion.58) | data formatting | bytes 1048576 | tf_op jit(solution)/shard_map/div | solution.py:92
  218.4 3.0 gather_fusion.4
  221.6 2.0 fusion.46
  224.9 4.9 %collective-permute-start.21 = (f32[2,2,32,128]{3,2,1,0:T(8,128)S(1)}, f32[2,2,32,128]{3,2,1,0:T(8,128)S(1)}, u32[]{:S(2)}, u32[]{:S(2)}) collective-permute-start(f32[2,2,32,128]{3,2,1,0:T(8,128)S(1)} %get-tuple-element.75), channel_id=1, source_target_pairs={{0,8},{8,16},{16,24},{1,9},{9,17},{17,25},{2,10},{10,18},{18,26},{... | collective-permute-start | bytes 196616 | tf_op jit(solution)/shard_map/ppermute | solution.py:27
  230.1 1.6 collective-permute-done.21
  233.0 6.9 %collective-permute-start.23 = (f32[2,20,2,128]{3,2,1,0:T(2,128)S(1)}, f32[2,20,2,128]{3,2,1,0:T(2,128)S(1)}, u32[]{:S(2)}, u32[]{:S(2)}) collective-permute-start(f32[2,20,2,128]{3,2,1,0:T(2,128)S(1)} %get-tuple-element.37), channel_id=1, source_target_pairs={{0,1},{1,2},{2,3},{3,4},{4,5},{5,6},{6,7},{8,9},{9,10},{10,11},{11... | collective-permute-start | bytes 122888 | tf_op jit(solution)/shard_map/ppermute | solution.py:27
  240.9 16.7 %copy.518 = f32[2,16,32,128]{0,3,2,1:T(8,128)} copy(f32[2,16,32,128]{3,2,1,0:T(8,128)S(1)} %fusion.46) | data formatting | bytes 1048576 | tf_op jit(solution)/shard_map/div | solution.py:92
  257.6 3.0 gather_fusion.5
  260.8 2.0 fusion.34
  264.1 4.9 %collective-permute-start.25 = (f32[2,2,32,128]{3,2,1,0:T(8,128)S(1)}, f32[2,2,32,128]{3,2,1,0:T(8,128)S(1)}, u32[]{:S(2)}, u32[]{:S(2)}) collective-permute-start(f32[2,2,32,128]{3,2,1,0:T(8,128)S(1)} %get-tuple-element.69), channel_id=1, source_target_pairs={{0,8},{8,16},{16,24},{1,9},{9,17},{17,25},{2,10},{10,18},{18,26},{... | collective-permute-start | bytes 196616 | tf_op jit(solution)/shard_map/ppermute | solution.py:27
  269.3 1.6 collective-permute-done.25
  272.2 6.9 %collective-permute-start.27 = (f32[2,20,2,128]{3,2,1,0:T(2,128)S(1)}, f32[2,20,2,128]{3,2,1,0:T(2,128)S(1)}, u32[]{:S(2)}, u32[]{:S(2)}) collective-permute-start(f32[2,20,2,128]{3,2,1,0:T(2,128)S(1)} %get-tuple-element.33), channel_id=1, source_target_pairs={{0,1},{1,2},{2,3},{3,4},{4,5},{5,6},{6,7},{8,9},{9,10},{10,11},{11... | collective-permute-start | bytes 122888 | tf_op jit(solution)/shard_map/ppermute | solution.py:27
  280.1 16.7 %copy.519 = f32[2,16,32,128]{0,3,2,1:T(8,128)} copy(f32[2,16,32,128]{3,2,1,0:T(8,128)S(1)} %fusion.34) | data formatting | bytes 1048576 | tf_op jit(solution)/shard_map/div | solution.py:92
  296.8 3.0 gather_fusion.6
  299.9 2.0 fusion.22
  303.2 4.9 %collective-permute-start.29 = (f32[2,2,32,128]{3,2,1,0:T(8,128)S(1)}, f32[2,2,32,128]{3,2,1,0:T(8,128)S(1)}, u32[]{:S(2)}, u32[]{:S(2)}) collective-permute-start(f32[2,2,32,128]{3,2,1,0:T(8,128)S(1)} %get-tuple-element.63), channel_id=1, source_target_pairs={{0,8},{8,16},{16,24},{1,9},{9,17},{17,25},{2,10},{10,18},{18,26},{... | collective-permute-start | bytes 196616 | tf_op jit(solution)/shard_map/ppermute | solution.py:27
  308.4 1.6 collective-permute-done.29
  311.3 7.2 %collective-permute-start.31 = (f32[2,20,2,128]{3,2,1,0:T(2,128)S(1)}, f32[2,20,2,128]{3,2,1,0:T(2,128)S(1)}, u32[]{:S(2)}, u32[]{:S(2)}) collective-permute-start(f32[2,20,2,128]{3,2,1,0:T(2,128)S(1)} %get-tuple-element.29), channel_id=1, source_target_pairs={{0,1},{1,2},{2,3},{3,4},{4,5},{5,6},{6,7},{8,9},{9,10},{10,11},{11... | collective-permute-start | bytes 122888 | tf_op jit(solution)/shard_map/ppermute | solution.py:27
  319.5 16.7 %copy.520 = f32[2,16,32,128]{0,3,2,1:T(8,128)} copy(f32[2,16,32,128]{3,2,1,0:T(8,128)S(1)} %fusion.22) | data formatting | bytes 1048576 | tf_op jit(solution)/shard_map/div | solution.py:92
  336.1 3.0 gather_fusion.7
  339.3 2.0 fusion.10
  341.3 16.8 %copy.521 = f32[2,16,32,128]{0,3,2,1:T(8,128)} copy(f32[2,16,32,128]{3,2,1,0:T(8,128)S(1)} %fusion.10) | data formatting | bytes 1048576 | tf_op jit(solution)/shard_map/div | solution.py:92
  358.1 2.4 gather_fusion.8
  360.5 1.4 bitcast_select_fusion
  362.6 97.4 %all-gather = f32[64,256,8]{1,2,0:T(8,128)S(1)} all-gather(f32[2,256,8]{1,2,0:T(8,128)S(1)} %stack.2), channel_id=2, replica_groups=mesh['shot'=4,'gx'=4,'gy'=8] {'gx','gy'}, dimensions={0}, use_global_device_ids=true | all-gather | bytes 540672 | tf_op jit(solution)/shard_map/all_gather | solution.py:14
  (125 shorter events, 29.4 us)
Async XLA Ops:
  7.2 97.1 %copy-start.1 = (f32[1,2,16,32,128]{4,3,2,1,0:T(8,128)S(1)}, f32[1,2,16,32,128]{4,3,2,1,0:T(8,128)}, u32[]{:S(2)}) copy-start(f32[1,2,16,32,128]{4,3,2,1,0:T(8,128)} %param.11) | copy-start | bytes 1572868
  7.2 54.9 %all-gather.3.cloned.1.call-start = ((), (), s32[]{:S(2)}) async-start(), calls=%async_computation | async-start | bytes 4456448 | tf_op jit(solution)/shard_map/all_gather | solution.py:119
  8.8 17.0 %collective-permute-start = (f32[2,2,32,128]{3,2,1,0:T(8,128)S(1)}, f32[2,2,32,128]{3,2,1,0:T(8,128)S(1)}, u32[]{:S(2)}, u32[]{:S(2)}) collective-permute-start(f32[2,2,32,128]{3,2,1,0:T(8,128)S(1)} %get-tuple-element.104), channel_id=1, source_target_pairs={{8,0},{16,8},{24,16},{9,1},{17,9},{25,17},{10,2},{18,10},{26,18},{... | collective-permute-start | bytes 196616 | tf_op jit(solution)/shard_map/ppermute | solution.py:29
  10.1 15.8 %collective-permute-start.1 = (f32[2,2,32,128]{3,2,1,0:T(8,128)S(1)}, f32[2,2,32,128]{3,2,1,0:T(8,128)S(1)}, u32[]{:S(2)}, u32[]{:S(2)}) collective-permute-start(f32[2,2,32,128]{3,2,1,0:T(8,128)S(1)} %get-tuple-element.105), channel_id=1, source_target_pairs={{0,8},{8,16},{16,24},{1,9},{9,17},{17,25},{2,10},{10,18},{18,26},{... | collective-permute-start | bytes 196616 | tf_op jit(solution)/shard_map/ppermute | solution.py:27
  25.8 39.0 %copy-start.3 = (f32[2,2,32,128]{3,2,1,0:T(8,128)}, f32[2,2,32,128]{3,2,1,0:T(8,128)S(1)}, u32[]{:S(2)}) copy-start(f32[2,2,32,128]{3,2,1,0:T(8,128)S(1)} %collective-permute-done) | copy-start | bytes 196612
  25.9 39.0 %copy-start.4 = (f32[2,2,32,128]{3,2,1,0:T(8,128)}, f32[2,2,32,128]{3,2,1,0:T(8,128)S(1)}, u32[]{:S(2)}) copy-start(f32[2,2,32,128]{3,2,1,0:T(8,128)S(1)} %collective-permute-done.1) | copy-start | bytes 196612
  26.9 7.7 %collective-permute-start.2 = (f32[2,20,2,128]{3,2,1,0:T(2,128)S(1)}, f32[2,20,2,128]{3,2,1,0:T(2,128)S(1)}, u32[]{:S(2)}, u32[]{:S(2)}) collective-permute-start(f32[2,20,2,128]{3,2,1,0:T(2,128)S(1)} %get-tuple-element.56), channel_id=1, source_target_pairs={{1,0},{2,1},{3,2},{4,3},{5,4},{6,5},{7,6},{9,8},{10,9},{11,10},{12... | collective-permute-start | bytes 122888 | tf_op jit(solution)/shard_map/ppermute | solution.py:29
  28.2 7.9 %collective-permute-start.3 = (f32[2,20,2,128]{3,2,1,0:T(2,128)S(1)}, f32[2,20,2,128]{3,2,1,0:T(2,128)S(1)}, u32[]{:S(2)}, u32[]{:S(2)}) collective-permute-start(f32[2,20,2,128]{3,2,1,0:T(2,128)S(1)} %get-tuple-element.57), channel_id=1, source_target_pairs={{0,1},{1,2},{2,3},{3,4},{4,5},{5,6},{6,7},{8,9},{9,10},{10,11},{11... | collective-permute-start | bytes 122888 | tf_op jit(solution)/shard_map/ppermute | solution.py:27
  68.1 6.8 %collective-permute-start.4 = (f32[2,2,32,128]{3,2,1,0:T(8,128)S(1)}, f32[2,2,32,128]{3,2,1,0:T(8,128)S(1)}, u32[]{:S(2)}, u32[]{:S(2)}) collective-permute-start(f32[2,2,32,128]{3,2,1,0:T(8,128)S(1)} %get-tuple-element.98), channel_id=1, source_target_pairs={{8,0},{16,8},{24,16},{9,1},{17,9},{25,17},{10,2},{18,10},{26,18},{... | collective-permute-start | bytes 196616 | tf_op jit(solution)/shard_map/ppermute | solution.py:29
  69.4 6.7 %collective-permute-start.5 = (f32[2,2,32,128]{3,2,1,0:T(8,128)S(1)}, f32[2,2,32,128]{3,2,1,0:T(8,128)S(1)}, u32[]{:S(2)}, u32[]{:S(2)}) collective-permute-start(f32[2,2,32,128]{3,2,1,0:T(8,128)S(1)} %get-tuple-element.99), channel_id=1, source_target_pairs={{0,8},{8,16},{16,24},{1,9},{9,17},{17,25},{2,10},{10,18},{18,26},{... | collective-permute-start | bytes 196616 | tf_op jit(solution)/shard_map/ppermute | solution.py:27
  76.0 28.2 %copy-start.11 = (f32[2,2,32,128]{3,2,1,0:T(8,128)}, f32[2,2,32,128]{3,2,1,0:T(8,128)S(1)}, u32[]{:S(2)}) copy-start(f32[2,2,32,128]{3,2,1,0:T(8,128)S(1)} %collective-permute-done.5) | copy-start | bytes 196612
  76.1 28.0 %collective-permute-start.6 = (f32[2,20,2,128]{3,2,1,0:T(2,128)S(1)}, f32[2,20,2,128]{3,2,1,0:T(2,128)S(1)}, u32[]{:S(2)}, u32[]{:S(2)}) collective-permute-start(f32[2,20,2,128]{3,2,1,0:T(2,128)S(1)} %get-tuple-element.52), channel_id=1, source_target_pairs={{1,0},{2,1},{3,2},{4,3},{5,4},{6,5},{7,6},{9,8},{10,9},{11,10},{12... | collective-permute-start | bytes 122888 | tf_op jit(solution)/shard_map/ppermute | solution.py:29
  77.4 26.7 %collective-permute-start.7 = (f32[2,20,2,128]{3,2,1,0:T(2,128)S(1)}, f32[2,20,2,128]{3,2,1,0:T(2,128)S(1)}, u32[]{:S(2)}, u32[]{:S(2)}) collective-permute-start(f32[2,20,2,128]{3,2,1,0:T(2,128)S(1)} %get-tuple-element.53), channel_id=1, source_target_pairs={{0,1},{1,2},{2,3},{3,4},{4,5},{5,6},{6,7},{8,9},{9,10},{10,11},{11... | collective-permute-start | bytes 122888 | tf_op jit(solution)/shard_map/ppermute | solution.py:27
  106.2 6.6 %collective-permute-start.8 = (f32[2,2,32,128]{3,2,1,0:T(8,128)S(1)}, f32[2,2,32,128]{3,2,1,0:T(8,128)S(1)}, u32[]{:S(2)}, u32[]{:S(2)}) collective-permute-start(f32[2,2,32,128]{3,2,1,0:T(8,128)S(1)} %get-tuple-element.92), channel_id=1, source_target_pairs={{8,0},{16,8},{24,16},{9,1},{17,9},{25,17},{10,2},{18,10},{26,18},{... | collective-permute-start | bytes 196616 | tf_op jit(solution)/shard_map/ppermute | solution.py:29
  107.5 6.9 %collective-permute-start.9 = (f32[2,2,32,128]{3,2,1,0:T(8,128)S(1)}, f32[2,2,32,128]{3,2,1,0:T(8,128)S(1)}, u32[]{:S(2)}, u32[]{:S(2)}) collective-permute-start(f32[2,2,32,128]{3,2,1,0:T(8,128)S(1)} %get-tuple-element.93), channel_id=1, source_target_pairs={{0,8},{8,16},{16,24},{1,9},{9,17},{17,25},{2,10},{10,18},{18,26},{... | collective-permute-start | bytes 196616 | tf_op jit(solution)/shard_map/ppermute | solution.py:27
  114.4 28.7 %copy-start.6 = (f32[2,2,32,128]{3,2,1,0:T(8,128)}, f32[2,2,32,128]{3,2,1,0:T(8,128)S(1)}, u32[]{:S(2)}) copy-start(f32[2,2,32,128]{3,2,1,0:T(8,128)S(1)} %collective-permute-done.9) | copy-start | bytes 196612
  114.5 28.5 %collective-permute-start.10 = (f32[2,20,2,128]{3,2,1,0:T(2,128)S(1)}, f32[2,20,2,128]{3,2,1,0:T(2,128)S(1)}, u32[]{:S(2)}, u32[]{:S(2)}) collective-permute-start(f32[2,20,2,128]{3,2,1,0:T(2,128)S(1)} %get-tuple-element.48), channel_id=1, source_target_pairs={{1,0},{2,1},{3,2},{4,3},{5,4},{6,5},{7,6},{9,8},{10,9},{11,10},{12... | collective-permute-start | bytes 122888 | tf_op jit(solution)/shard_map/ppermute | solution.py:29
  115.8 27.2 %collective-permute-start.11 = (f32[2,20,2,128]{3,2,1,0:T(2,128)S(1)}, f32[2,20,2,128]{3,2,1,0:T(2,128)S(1)}, u32[]{:S(2)}, u32[]{:S(2)}) collective-permute-start(f32[2,20,2,128]{3,2,1,0:T(2,128)S(1)} %get-tuple-element.49), channel_id=1, source_target_pairs={{0,1},{1,2},{2,3},{3,4},{4,5},{5,6},{6,7},{8,9},{9,10},{10,11},{11... | collective-permute-start | bytes 122888 | tf_op jit(solution)/shard_map/ppermute | solution.py:27
  145.1 6.5 %collective-permute-start.12 = (f32[2,2,32,128]{3,2,1,0:T(8,128)S(1)}, f32[2,2,32,128]{3,2,1,0:T(8,128)S(1)}, u32[]{:S(2)}, u32[]{:S(2)}) collective-permute-start(f32[2,2,32,128]{3,2,1,0:T(8,128)S(1)} %get-tuple-element.86), channel_id=1, source_target_pairs={{8,0},{16,8},{24,16},{9,1},{17,9},{25,17},{10,2},{18,10},{26,18},{... | collective-permute-start | bytes 196616 | tf_op jit(solution)/shard_map/ppermute | solution.py:29
  146.4 6.8 %collective-permute-start.13 = (f32[2,2,32,128]{3,2,1,0:T(8,128)S(1)}, f32[2,2,32,128]{3,2,1,0:T(8,128)S(1)}, u32[]{:S(2)}, u32[]{:S(2)}) collective-permute-start(f32[2,2,32,128]{3,2,1,0:T(8,128)S(1)} %get-tuple-element.87), channel_id=1, source_target_pairs={{0,8},{8,16},{16,24},{1,9},{9,17},{17,25},{2,10},{10,18},{18,26},{... | collective-permute-start | bytes 196616 | tf_op jit(solution)/shard_map/ppermute | solution.py:27
  153.2 29.1 %copy-start.7 = (f32[2,2,32,128]{3,2,1,0:T(8,128)}, f32[2,2,32,128]{3,2,1,0:T(8,128)S(1)}, u32[]{:S(2)}) copy-start(f32[2,2,32,128]{3,2,1,0:T(8,128)S(1)} %collective-permute-done.13) | copy-start | bytes 196612
  153.2 28.9 %collective-permute-start.14 = (f32[2,20,2,128]{3,2,1,0:T(2,128)S(1)}, f32[2,20,2,128]{3,2,1,0:T(2,128)S(1)}, u32[]{:S(2)}, u32[]{:S(2)}) collective-permute-start(f32[2,20,2,128]{3,2,1,0:T(2,128)S(1)} %get-tuple-element.44), channel_id=1, source_target_pairs={{1,0},{2,1},{3,2},{4,3},{5,4},{6,5},{7,6},{9,8},{10,9},{11,10},{12... | collective-permute-start | bytes 122888 | tf_op jit(solution)/shard_map/ppermute | solution.py:29
  154.5 27.6 %collective-permute-start.15 = (f32[2,20,2,128]{3,2,1,0:T(2,128)S(1)}, f32[2,20,2,128]{3,2,1,0:T(2,128)S(1)}, u32[]{:S(2)}, u32[]{:S(2)}) collective-permute-start(f32[2,20,2,128]{3,2,1,0:T(2,128)S(1)} %get-tuple-element.45), channel_id=1, source_target_pairs={{0,1},{1,2},{2,3},{3,4},{4,5},{5,6},{6,7},{8,9},{9,10},{10,11},{11... | collective-permute-start | bytes 122888 | tf_op jit(solution)/shard_map/ppermute | solution.py:27
  184.3 6.5 %collective-permute-start.16 = (f32[2,2,32,128]{3,2,1,0:T(8,128)S(1)}, f32[2,2,32,128]{3,2,1,0:T(8,128)S(1)}, u32[]{:S(2)}, u32[]{:S(2)}) collective-permute-start(f32[2,2,32,128]{3,2,1,0:T(8,128)S(1)} %get-tuple-element.80), channel_id=1, source_target_pairs={{8,0},{16,8},{24,16},{9,1},{17,9},{25,17},{10,2},{18,10},{26,18},{... | collective-permute-start | bytes 196616 | tf_op jit(solution)/shard_map/ppermute | solution.py:29
  185.6 6.8 %collective-permute-start.17 = (f32[2,2,32,128]{3,2,1,0:T(8,128)S(1)}, f32[2,2,32,128]{3,2,1,0:T(8,128)S(1)}, u32[]{:S(2)}, u32[]{:S(2)}) collective-permute-start(f32[2,2,32,128]{3,2,1,0:T(8,128)S(1)} %get-tuple-element.81), channel_id=1, source_target_pairs={{0,8},{8,16},{16,24},{1,9},{9,17},{17,25},{2,10},{10,18},{18,26},{... | collective-permute-start | bytes 196616 | tf_op jit(solution)/shard_map/ppermute | solution.py:27
  192.3 29.3 %copy-start.8 = (f32[2,2,32,128]{3,2,1,0:T(8,128)}, f32[2,2,32,128]{3,2,1,0:T(8,128)S(1)}, u32[]{:S(2)}) copy-start(f32[2,2,32,128]{3,2,1,0:T(8,128)S(1)} %collective-permute-done.17) | copy-start | bytes 196612
  192.4 29.1 %collective-permute-start.18 = (f32[2,20,2,128]{3,2,1,0:T(2,128)S(1)}, f32[2,20,2,128]{3,2,1,0:T(2,128)S(1)}, u32[]{:S(2)}, u32[]{:S(2)}) collective-permute-start(f32[2,20,2,128]{3,2,1,0:T(2,128)S(1)} %get-tuple-element.40), channel_id=1, source_target_pairs={{1,0},{2,1},{3,2},{4,3},{5,4},{6,5},{7,6},{9,8},{10,9},{11,10},{12... | collective-permute-start | bytes 122888 | tf_op jit(solution)/shard_map/ppermute | solution.py:29
  193.7 27.8 %collective-permute-start.19 = (f32[2,20,2,128]{3,2,1,0:T(2,128)S(1)}, f32[2,20,2,128]{3,2,1,0:T(2,128)S(1)}, u32[]{:S(2)}, u32[]{:S(2)}) collective-permute-start(f32[2,20,2,128]{3,2,1,0:T(2,128)S(1)} %get-tuple-element.41), channel_id=1, source_target_pairs={{0,1},{1,2},{2,3},{3,4},{4,5},{5,6},{6,7},{8,9},{9,10},{10,11},{11... | collective-permute-start | bytes 122888 | tf_op jit(solution)/shard_map/ppermute | solution.py:27
  223.6 6.5 %collective-permute-start.20 = (f32[2,2,32,128]{3,2,1,0:T(8,128)S(1)}, f32[2,2,32,128]{3,2,1,0:T(8,128)S(1)}, u32[]{:S(2)}, u32[]{:S(2)}) collective-permute-start(f32[2,2,32,128]{3,2,1,0:T(8,128)S(1)} %get-tuple-element.74), channel_id=1, source_target_pairs={{8,0},{16,8},{24,16},{9,1},{17,9},{25,17},{10,2},{18,10},{26,18},{... | collective-permute-start | bytes 196616 | tf_op jit(solution)/shard_map/ppermute | solution.py:29
  224.9 6.8 %collective-permute-start.21 = (f32[2,2,32,128]{3,2,1,0:T(8,128)S(1)}, f32[2,2,32,128]{3,2,1,0:T(8,128)S(1)}, u32[]{:S(2)}, u32[]{:S(2)}) collective-permute-start(f32[2,2,32,128]{3,2,1,0:T(8,128)S(1)} %get-tuple-element.75), channel_id=1, source_target_pairs={{0,8},{8,16},{16,24},{1,9},{9,17},{17,25},{2,10},{10,18},{18,26},{... | collective-permute-start | bytes 196616 | tf_op jit(solution)/shard_map/ppermute | solution.py:27
  231.7 29.1 %copy-start.9 = (f32[2,2,32,128]{3,2,1,0:T(8,128)}, f32[2,2,32,128]{3,2,1,0:T(8,128)S(1)}, u32[]{:S(2)}) copy-start(f32[2,2,32,128]{3,2,1,0:T(8,128)S(1)} %collective-permute-done.21) | copy-start | bytes 196612
  231.7 28.9 %collective-permute-start.22 = (f32[2,20,2,128]{3,2,1,0:T(2,128)S(1)}, f32[2,20,2,128]{3,2,1,0:T(2,128)S(1)}, u32[]{:S(2)}, u32[]{:S(2)}) collective-permute-start(f32[2,20,2,128]{3,2,1,0:T(2,128)S(1)} %get-tuple-element.36), channel_id=1, source_target_pairs={{1,0},{2,1},{3,2},{4,3},{5,4},{6,5},{7,6},{9,8},{10,9},{11,10},{12... | collective-permute-start | bytes 122888 | tf_op jit(solution)/shard_map/ppermute | solution.py:29
  233.0 27.6 %collective-permute-start.23 = (f32[2,20,2,128]{3,2,1,0:T(2,128)S(1)}, f32[2,20,2,128]{3,2,1,0:T(2,128)S(1)}, u32[]{:S(2)}, u32[]{:S(2)}) collective-permute-start(f32[2,20,2,128]{3,2,1,0:T(2,128)S(1)} %get-tuple-element.37), channel_id=1, source_target_pairs={{0,1},{1,2},{2,3},{3,4},{4,5},{5,6},{6,7},{8,9},{9,10},{10,11},{11... | collective-permute-start | bytes 122888 | tf_op jit(solution)/shard_map/ppermute | solution.py:27
  262.8 6.5 %collective-permute-start.24 = (f32[2,2,32,128]{3,2,1,0:T(8,128)S(1)}, f32[2,2,32,128]{3,2,1,0:T(8,128)S(1)}, u32[]{:S(2)}, u32[]{:S(2)}) collective-permute-start(f32[2,2,32,128]{3,2,1,0:T(8,128)S(1)} %get-tuple-element.68), channel_id=1, source_target_pairs={{8,0},{16,8},{24,16},{9,1},{17,9},{25,17},{10,2},{18,10},{26,18},{... | collective-permute-start | bytes 196616 | tf_op jit(solution)/shard_map/ppermute | solution.py:29
  264.1 6.8 %collective-permute-start.25 = (f32[2,2,32,128]{3,2,1,0:T(8,128)S(1)}, f32[2,2,32,128]{3,2,1,0:T(8,128)S(1)}, u32[]{:S(2)}, u32[]{:S(2)}) collective-permute-start(f32[2,2,32,128]{3,2,1,0:T(8,128)S(1)} %get-tuple-element.69), channel_id=1, source_target_pairs={{0,8},{8,16},{16,24},{1,9},{9,17},{17,25},{2,10},{10,18},{18,26},{... | collective-permute-start | bytes 196616 | tf_op jit(solution)/shard_map/ppermute | solution.py:27
  270.8 29.1 %copy-start.10 = (f32[2,2,32,128]{3,2,1,0:T(8,128)}, f32[2,2,32,128]{3,2,1,0:T(8,128)S(1)}, u32[]{:S(2)}) copy-start(f32[2,2,32,128]{3,2,1,0:T(8,128)S(1)} %collective-permute-done.25) | copy-start | bytes 196612
  270.9 28.9 %collective-permute-start.26 = (f32[2,20,2,128]{3,2,1,0:T(2,128)S(1)}, f32[2,20,2,128]{3,2,1,0:T(2,128)S(1)}, u32[]{:S(2)}, u32[]{:S(2)}) collective-permute-start(f32[2,20,2,128]{3,2,1,0:T(2,128)S(1)} %get-tuple-element.32), channel_id=1, source_target_pairs={{1,0},{2,1},{3,2},{4,3},{5,4},{6,5},{7,6},{9,8},{10,9},{11,10},{12... | collective-permute-start | bytes 122888 | tf_op jit(solution)/shard_map/ppermute | solution.py:29
  272.2 27.6 %collective-permute-start.27 = (f32[2,20,2,128]{3,2,1,0:T(2,128)S(1)}, f32[2,20,2,128]{3,2,1,0:T(2,128)S(1)}, u32[]{:S(2)}, u32[]{:S(2)}) collective-permute-start(f32[2,20,2,128]{3,2,1,0:T(2,128)S(1)} %get-tuple-element.33), channel_id=1, source_target_pairs={{0,1},{1,2},{2,3},{3,4},{4,5},{5,6},{6,7},{8,9},{9,10},{10,11},{11... | collective-permute-start | bytes 122888 | tf_op jit(solution)/shard_map/ppermute | solution.py:27
  301.9 56.2 %copy-start = (f32[2,16,32,128]{3,2,1,0:T(8,128)}, f32[2,16,32,128]{3,2,1,0:T(8,128)S(1)}, u32[]{:S(2)}) copy-start(f32[2,16,32,128]{3,2,1,0:T(8,128)S(1)} %fusion.22) | copy-start | bytes 1572868
  301.9 6.5 %collective-permute-start.28 = (f32[2,2,32,128]{3,2,1,0:T(8,128)S(1)}, f32[2,2,32,128]{3,2,1,0:T(8,128)S(1)}, u32[]{:S(2)}, u32[]{:S(2)}) collective-permute-start(f32[2,2,32,128]{3,2,1,0:T(8,128)S(1)} %get-tuple-element.62), channel_id=1, source_target_pairs={{8,0},{16,8},{24,16},{9,1},{17,9},{25,17},{10,2},{18,10},{26,18},{... | collective-permute-start | bytes 196616 | tf_op jit(solution)/shard_map/ppermute | solution.py:29
  303.2 6.8 %collective-permute-start.29 = (f32[2,2,32,128]{3,2,1,0:T(8,128)S(1)}, f32[2,2,32,128]{3,2,1,0:T(8,128)S(1)}, u32[]{:S(2)}, u32[]{:S(2)}) collective-permute-start(f32[2,2,32,128]{3,2,1,0:T(8,128)S(1)} %get-tuple-element.63), channel_id=1, source_target_pairs={{0,8},{8,16},{16,24},{1,9},{9,17},{17,25},{2,10},{10,18},{18,26},{... | collective-permute-start | bytes 196616 | tf_op jit(solution)/shard_map/ppermute | solution.py:27
  310.0 29.3 %copy-start.5 = (f32[2,2,32,128]{3,2,1,0:T(8,128)}, f32[2,2,32,128]{3,2,1,0:T(8,128)S(1)}, u32[]{:S(2)}) copy-start(f32[2,2,32,128]{3,2,1,0:T(8,128)S(1)} %collective-permute-done.29) | copy-start | bytes 196612
  310.0 29.1 %collective-permute-start.30 = (f32[2,20,2,128]{3,2,1,0:T(2,128)S(1)}, f32[2,20,2,128]{3,2,1,0:T(2,128)S(1)}, u32[]{:S(2)}, u32[]{:S(2)}) collective-permute-start(f32[2,20,2,128]{3,2,1,0:T(2,128)S(1)} %get-tuple-element.28), channel_id=1, source_target_pairs={{1,0},{2,1},{3,2},{4,3},{5,4},{6,5},{7,6},{9,8},{10,9},{11,10},{12... | collective-permute-start | bytes 122888 | tf_op jit(solution)/shard_map/ppermute | solution.py:29
  311.3 27.8 %collective-permute-start.31 = (f32[2,20,2,128]{3,2,1,0:T(2,128)S(1)}, f32[2,20,2,128]{3,2,1,0:T(2,128)S(1)}, u32[]{:S(2)}, u32[]{:S(2)}) collective-permute-start(f32[2,20,2,128]{3,2,1,0:T(2,128)S(1)} %get-tuple-element.29), channel_id=1, source_target_pairs={{0,1},{1,2},{2,3},{3,4},{4,5},{5,6},{6,7},{8,9},{9,10},{10,11},{11... | collective-permute-start | bytes 122888 | tf_op jit(solution)/shard_map/ppermute | solution.py:27
  341.3 119.4 %copy-start.2 = (f32[2,16,32,128]{3,2,1,0:T(8,128)}, f32[2,16,32,128]{3,2,1,0:T(8,128)S(1)}, u32[]{:S(2)}) copy-start(f32[2,16,32,128]{3,2,1,0:T(8,128)S(1)} %fusion.10) | copy-start | bytes 1572868
  341.3 19.2 %copy-start.12 = (f32[256,2]{1,0:T(8,128)S(1)}, f32[256,2]{1,0:T(8,128)}, u32[]{:S(2)}) copy-start(f32[256,2]{1,0:T(8,128)} %gather_fusion.7) | copy-start | bytes 6148
Sparse Core Ops, SparseCore 0:
  9.7 52.3 all-gather.2
